TPU v7x, 32 devices: a whole 2x2x4 slice. The times are simulated.
32 devices in a mesh: groups: 2 (over y), space: 4 (over z), dp: 2 (over x), ysp: 2 (over core).
Axes of the slice: x: 2, y: 2, z: 4, core: 2. Of those that a mesh axis runs over, the one named last changes fastest.
Arguments:
- inputs: bfloat16 [4, 8, 16, 2048], P(('groups', 'dp'), 'space', 'ysp'), parts along dimension 0, may hold values from -6 to 6
- w_first: float32 [864, 64], replicated, may hold values from -0.21875 to 0.21875
- b_first: float32 [64], replicated, may hold values from -2 to 2
- w_second: float32 [1728, 64], replicated, may hold values from -0.15625 to 0.15625
- b_second: float32 [64], replicated, may hold values from -2 to 2
- cotangent: bfloat16 [4, 8, 16, 4096], P(('groups', 'dp'), 'space', 'ysp'), parts along dimension 0, may hold values from -16 to 16
Outputs:
- output: bfloat16 [4, 8, 16, 4096], P(('groups', 'dp'), 'space', 'ysp'), parts along dimension 0
- input_grad: bfloat16 [4, 8, 16, 2048], P(('groups', 'dp'), 'space', 'ysp'), parts along dimension 0
- grad_w_first: float32 [1728, 64], P('groups'), parts along dimension 0
- grad_b_first: float32 [128], P('groups'), parts along dimension 0
- grad_w_second: float32 [3456, 64], P('groups'), parts along dimension 0
- grad_b_second: float32 [128], P('groups'), parts along dimension 0
There are 2 independent parts, one for each index of `groups`. A program takes and returns all parts, laid end to end along the dimension named above; an argument that names none is the same for every part. Nothing has to cross between parts.
All inputs are finite; a program needn't handle non-finite values.
Results may differ from a plain program's by a relative error of at most 0.0075.
Values may be sent and summed in bfloat16 or wider, within the bound.
No kernel may reach another device: no remote copies, remote signals or barrier semaphores. Data moves between devices by JAX's collectives and lax.ppermute only.
A program may use at most 64 MiB of HBM per device.

v0:
```python
import jax
import jax.numpy as jnp
from jax import lax
from jax.sharding import PartitionSpec as P

C_IN = 32
C_MID = 64
DEPTH = 64


def padded_2(cells, sides, width):
    for axis, dim in sides:
        count = lax.axis_size(axis)
        ends = count - 1
        head = lax.slice_in_dim(cells, 0, width, axis=dim)
        tail = lax.slice_in_dim(cells, cells.shape[dim] - width, cells.shape[dim], axis=dim)
        cells = jnp.concatenate(
            [
                lax.ppermute(tail, axis, [(i, (i + 1) % count) for i in range(ends)]),
                cells,
                lax.ppermute(head, axis, [((i + 1) % count, i) for i in range(ends)]),
            ],
            axis=dim,
        )
    return cells


def columns(padded, chans):
    batch = padded.shape[0]
    wide_x = padded.shape[1] - 2
    wide_y = padded.shape[2] - 2
    cells = padded.reshape(batch, wide_x + 2, wide_y + 2, DEPTH, chans)
    cells = jnp.pad(cells, ((0, 0), (0, 0), (0, 0), (1, 1), (0, 0)))
    pieces = []
    for first in range(3):
        for second in range(3):
            for third in range(3):
                pieces.append(
                    cells[
                        :,
                        first : first + wide_x,
                        second : second + wide_y,
                        third : third + DEPTH,
                        :,
                    ]
                )
    return jnp.concatenate(pieces, axis=-1).reshape(-1, 27 * chans)


def flipped(weights, chans_in, chans_out):
    cube = weights.reshape(3, 3, 3, chans_in, chans_out)[::-1, ::-1, ::-1]
    return jnp.transpose(cube, (0, 1, 2, 4, 3)).reshape(27 * chans_out, chans_in)


def silu_grad(value):
    sig = jax.nn.sigmoid(value)
    return sig * (1.0 + value * (1.0 - sig))


def weight_term(patches, grads):
    return lax.dot_general(
        patches, grads, (((0,), (0,)), ((), ())), preferred_element_type=jnp.float32
    )


def on_device(inputs, w_first, b_first, w_second, b_second, cotangent):
    batch, cells_x, cells_y = (inputs.shape[0], inputs.shape[1], inputs.shape[2])
    w1_round = w_first.astype(jnp.bfloat16)
    w2_round = w_second.astype(jnp.bfloat16)
    in_padded = padded_2(inputs, (("space", 1), ("ysp", 2)), 1)
    first_cols = columns(in_padded, C_IN)
    y_first = jnp.dot(first_cols, w1_round, preferred_element_type=jnp.float32) + b_first
    act_first = (
        jax.nn.silu(y_first).astype(jnp.bfloat16).reshape(batch, cells_x, cells_y, DEPTH * C_MID)
    )
    mid_padded = padded_2(act_first, (("space", 1), ("ysp", 2)), 1)
    second_cols = columns(mid_padded, C_MID)
    y_second = jnp.dot(second_cols, w2_round, preferred_element_type=jnp.float32) + b_second
    output = (
        jax.nn.silu(y_second).astype(jnp.bfloat16).reshape(batch, cells_x, cells_y, DEPTH * C_MID)
    )
    g_second = (cotangent.reshape(-1, C_MID).astype(jnp.float32) * silu_grad(y_second)).astype(
        jnp.bfloat16
    )
    grad_w2 = weight_term(second_cols, g_second)
    grad_b2 = jnp.sum(g_second.astype(jnp.float32), axis=0)
    g2_padded = padded_2(
        g_second.reshape(batch, cells_x, cells_y, DEPTH * C_MID), (("space", 1), ("ysp", 2)), 1
    )
    d_first = jnp.dot(
        columns(g2_padded, C_MID),
        flipped(w2_round, C_MID, C_MID),
        preferred_element_type=jnp.float32,
    )
    g_first = (d_first * silu_grad(y_first)).astype(jnp.bfloat16)
    grad_w1 = weight_term(first_cols, g_first)
    grad_b1 = jnp.sum(g_first.astype(jnp.float32), axis=0)
    g1_padded = padded_2(
        g_first.reshape(batch, cells_x, cells_y, DEPTH * C_MID), (("space", 1), ("ysp", 2)), 1
    )
    d_input = jnp.dot(
        columns(g1_padded, C_MID),
        flipped(w1_round, C_IN, C_MID),
        preferred_element_type=jnp.float32,
    )
    input_grad = d_input.astype(jnp.bfloat16).reshape(batch, cells_x, cells_y, DEPTH * C_IN)
    grad_w1, grad_b1, grad_w2, grad_b2 = lax.psum(
        (grad_w1, grad_b1, grad_w2, grad_b2), ("space", "dp", "ysp")
    )
    return (output, input_grad, grad_w1, grad_b1, grad_w2, grad_b2)


def solution(mesh):
    placed = (
        P(("groups", "dp"), "space", "ysp", None),
        P(),
        P(),
        P(),
        P(),
        P(("groups", "dp"), "space", "ysp", None),
    )
    return jax.shard_map(
        on_device,
        mesh=mesh,
        in_specs=placed,
        out_specs=(
            P(("groups", "dp"), "space", "ysp", None),
            P(("groups", "dp"), "space", "ysp", None),
            P("groups", None),
            P("groups"),
            P("groups", None),
            P("groups"),
        ),
        check_vma=False,
    )
```

profile of v0, /device:TPU:0, one launch (start us, length us, event | category | flops | bytes accessed | tf_op | source)
XLA Modules:
  0.0 233.7 jit_solution(10804659027833530314)
XLA Ops:
  8.0 4.9 %collective-permute-start = (bf16[1,1,8,2048]{3,2,1,0:T(8,128)(2,1)S(1)}, bf16[1,1,8,2048]{3,2,1,0:T(8,128)(2,1)S(1)}, u32[]{:S(2)}, u32[]{:S(2)}) collective-permute-start(bf16[1,1,8,2048]{3,2,1,0:T(8,128)(2,1)S(1)} %get-tuple-element.136), channel_id=1, source_target_pairs={{0,4},{4,8},{8,12},{1,5},{5,9},{9,13},{2,6},{6,10},{10,14},{3,7},{... | collective-permute-start | bytes 98312 | tf_op jit(solution)/shard_map/ppermute | solution.py:19
  12.9 1.3 collective-permute-start.1
  15.3 3.4 %collective-permute-done.1 = bf16[1,1,8,2048]{3,2,1,0:T(8,128)(2,1)S(1)} collective-permute-done((bf16[1,1,8,2048]{3,2,1,0:T(8,128)(2,1)S(1)}, bf16[1,1,8,2048]{3,2,1,0:T(8,128)(2,1)S(1)}, u32[]{:S(2)}, u32[]{:S(2)}) %collective-permute-start.1) | collective-permute-done | bytes 32800 | tf_op jit(solution)/shard_map/ppermute | solution.py:21
  18.8 1.3 collective-permute-start.2
  20.1 1.3 collective-permute-start.3
  21.4 1.8 copy.27
  24.2 1.6 pad_slice_fusion.54
  25.8 1.8 pad_slice_fusion.55
  27.5 8.3 %concatenate.38 = bf16[1,2,8,64,864]{4,3,1,2,0:T(8,128)(2,1)} concatenate(bf16[1,2,8,64,32]{4,3,1,2,0:T(8,128)(2,1)S(1)} %get-tuple-element.119, bf16[1,2,8,64,32]{4,3,1,2,0:T(8,128)(2,1)S(1)} %get-tuple-element.118, bf16[1,2,8,64,32]{4,3,1,2,0:T(8,128)(2,1)S(1)} %get-tuple-element.94, bf16[1,2,8,64,32]{4,3,1,2,0:T(8,128)(2,1)S(1)} %get-tuple-element.95, ...), dimensions={4} | concatenate | bytes 3538944 | tf_op jit(solution)/shard_map/concatenate | solution.py:47
  35.9 1.7 copy.26
  37.7 1.4 multiply_convert_fusion.2
  39.6 3.5 %collective-permute-start.4 = (bf16[1,1,8,4096]{3,2,1,0:T(8,128)(2,1)S(1)}, bf16[1,1,8,4096]{3,2,1,0:T(8,128)(2,1)S(1)}, u32[]{:S(2)}, u32[]{:S(2)}) collective-permute-start(bf16[1,1,8,4096]{3,2,1,0:T(8,128)(2,1)S(1)} %get-tuple-element.132), channel_id=1, source_target_pairs={{0,4},{4,8},{8,12},{1,5},{5,9},{9,13},{2,6},{6,10},{10,14},{3,7},{... | collective-permute-start | bytes 196616 | tf_op jit(solution)/shard_map/ppermute | solution.py:19
  43.1 1.3 collective-permute-start.5
  45.4 4.4 %collective-permute-done.5 = bf16[1,1,8,4096]{3,2,1,0:T(8,128)(2,1)S(1)} collective-permute-done((bf16[1,1,8,4096]{3,2,1,0:T(8,128)(2,1)S(1)}, bf16[1,1,8,4096]{3,2,1,0:T(8,128)(2,1)S(1)}, u32[]{:S(2)}, u32[]{:S(2)}) %collective-permute-start.5) | collective-permute-done | bytes 65568 | tf_op jit(solution)/shard_map/ppermute | solution.py:21
  49.9 1.9 collective-permute-start.6
  51.8 1.3 collective-permute-start.7
  56.0 1.2 fusion.3
  57.2 1.9 pad_slice_fusion.36
  59.0 1.8 pad_slice_fusion.37
  60.8 8.8 %concatenate.41 = bf16[1,2,8,64,1728]{4,3,1,2,0:T(8,128)(2,1)} concatenate(bf16[1,2,8,64,64]{4,3,1,2,0:T(8,128)(2,1)} %get-tuple-element.92, bf16[1,2,8,64,64]{4,3,1,2,0:T(8,128)(2,1)} %get-tuple-element.91, bf16[1,2,8,64,64]{4,3,1,2,0:T(8,128)(2,1)} %get-tuple-element.67, bf16[1,2,8,64,64]{4,3,1,2,0:T(8,128)(2,1)} %get-tuple-element.68, ...), dimensions={4} | concatenate | bytes 7077888 | tf_op jit(solution)/shard_map/concatenate | solution.py:47
  69.7 2.4 %copy.30 = bf16[1,2,8,64,1728]{4,3,2,1,0:T(8,128)(2,1)S(1)} copy(bf16[1,2,8,64,1728]{4,3,1,2,0:T(8,128)(2,1)} %concatenate.41) | data formatting | bytes 7077888 | tf_op jit(solution)/shard_map/concatenate | solution.py:47
  72.2 2.0 convert_reduce_fusion
  75.4 3.5 %collective-permute-start.8 = (bf16[1,1,8,4096]{3,2,1,0:T(8,128)(2,1)S(1)}, bf16[1,1,8,4096]{3,2,1,0:T(8,128)(2,1)S(1)}, u32[]{:S(2)}, u32[]{:S(2)}) collective-permute-start(bf16[1,1,8,4096]{3,2,1,0:T(8,128)(2,1)S(1)} %get-tuple-element.130), channel_id=1, source_target_pairs={{0,4},{4,8},{8,12},{1,5},{5,9},{9,13},{2,6},{6,10},{10,14},{3,7},{... | collective-permute-start | bytes 196616 | tf_op jit(solution)/shard_map/ppermute | solution.py:19
  78.8 1.3 collective-permute-start.9
  81.2 4.4 %collective-permute-done.9 = bf16[1,1,8,4096]{3,2,1,0:T(8,128)(2,1)S(1)} collective-permute-done((bf16[1,1,8,4096]{3,2,1,0:T(8,128)(2,1)S(1)}, bf16[1,1,8,4096]{3,2,1,0:T(8,128)(2,1)S(1)}, u32[]{:S(2)}, u32[]{:S(2)}) %collective-permute-start.9) | collective-permute-done | bytes 65568 | tf_op jit(solution)/shard_map/ppermute | solution.py:21
  86.3 1.9 collective-permute-start.10
  88.2 1.5 collective-permute-start.11
  91.1 1.7 rev.6
  96.0 1.2 fusion.2
  97.2 1.8 pad_slice_fusion.18
  99.1 1.8 pad_slice_fusion.19
  100.8 8.8 %concatenate.44 = bf16[1,2,8,64,1728]{4,3,1,2,0:T(8,128)(2,1)} concatenate(bf16[1,2,8,64,64]{4,3,1,2,0:T(8,128)(2,1)} %get-tuple-element.65, bf16[1,2,8,64,64]{4,3,1,2,0:T(8,128)(2,1)} %get-tuple-element.64, bf16[1,2,8,64,64]{4,3,1,2,0:T(8,128)(2,1)} %get-tuple-element.40, bf16[1,2,8,64,64]{4,3,1,2,0:T(8,128)(2,1)} %get-tuple-element.41, ...), dimensions={4} | concatenate | bytes 7077888 | tf_op jit(solution)/shard_map/concatenate | solution.py:47
  109.7 2.4 %copy.35 = bf16[1,2,8,64,1728]{4,3,2,1,0:T(8,128)(2,1)S(1)} copy(bf16[1,2,8,64,1728]{4,3,1,2,0:T(8,128)(2,1)} %concatenate.44) | data formatting | bytes 7077888 | tf_op jit(solution)/shard_map/concatenate | solution.py:47
  112.2 1.3 convert_reduce_fusion.1
  114.0 2.3 collective-permute-start.12
  116.3 3.6 %fusion.14 = f32[1728,64]{0,1:T(8,128)} fusion(bf16[1024,64]{0,1:T(8,128)(2,1)S(1)} %copy-done.5, bf16[1024,1728]{1,0:T(8,128)(2,1)} %bitcast.38), kind=kOutput, calls=%fused_computation.114 | convolution fusion | flops 226492416 | bytes 4112384 | tf_op jit(solution)/shard_map/dot_general | solution.py:61
  121.0 1.3 collective-permute-start.13
  122.3 5.4 %collective-permute-done.13 = bf16[1,1,8,4096]{3,2,1,0:T(8,128)(2,1)S(1)} collective-permute-done((bf16[1,1,8,4096]{3,2,1,0:T(8,128)(2,1)S(1)}, bf16[1,1,8,4096]{3,2,1,0:T(8,128)(2,1)S(1)}, u32[]{:S(2)}, u32[]{:S(2)}) %collective-permute-start.13) | collective-permute-done | bytes 65568 | tf_op jit(solution)/shard_map/ppermute | solution.py:21
  127.8 1.9 collective-permute-start.14
  129.7 1.3 collective-permute-start.15
  132.1 31.3 %all-reduce.4 = (f32[64]{0:T(128)}, f32[64]{0:T(128)}) all-reduce(f32[64]{0:T(128)S(1)} %get-tuple-element.139, f32[64]{0:T(128)S(1)} %get-tuple-element.10), channel_id=1, replica_groups=mesh['groups'=2,'space'=4,'dp'=2,'ysp'=2] {'space','dp','ysp'}, use_global_device_ids=true, to_apply=%region_2.3 | all-reduce | flops 128 | bytes 1024 | tf_op jit(solution)/shard_map/psum | solution.py:107
  165.2 1.7 pad_slice_fusion.1
  167.0 1.3 fusion.1
  168.3 9.0 %concatenate.47 = bf16[1,2,8,64,1728]{4,3,1,2,0:T(8,128)(2,1)} concatenate(bf16[1,2,8,64,64]{4,3,1,2,0:T(8,128)(2,1)} %get-tuple-element.38, bf16[1,2,8,64,64]{4,3,1,2,0:T(8,128)(2,1)} %get-tuple-element.37, bf16[1,2,8,64,64]{4,3,1,2,0:T(8,128)(2,1)S(1)} %get-tuple-element.13, bf16[1,2,8,64,64]{4,3,1,2,0:T(8,128)(2,1)S(1)} %get-tuple-element.14, ...), dimensions={4} | concatenate | bytes 7077888 | tf_op jit(solution)/shard_map/concatenate | solution.py:47
  177.3 2.4 %copy.39 = bf16[1,2,8,64,1728]{4,3,2,1,0:T(8,128)(2,1)S(1)} copy(bf16[1,2,8,64,1728]{4,3,1,2,0:T(8,128)(2,1)} %concatenate.47) | data formatting | bytes 7077888 | tf_op jit(solution)/shard_map/concatenate | solution.py:47
  181.9 41.4 %all-reduce.8.cloned.1.call-done = (f32[864,64]{0,1:T(8,128)}, f32[1728,64]{0,1:T(8,128)}) async-done(((f32[864,64]{0,1:T(8,128)}, f32[1728,64]{0,1:T(8,128)}), (f32[864,64]{0,1:T(8,128)}, f32[1728,64]{0,1:T(8,128)})) %all-reduce.8.cloned.1.call-update) | async-done | bytes 663568 | tf_op jit(solution)/shard_map/psum | solution.py:107
  223.4 1.6 copy.52
  225.0 1.8 copy.53
  (99 shorter events, 21.8 us)
Async XLA Ops:
  7.2 216.2 %all-reduce.8.cloned.1.call-start = ((), (), s32[]{:S(2)}) async-start(), calls=%async_computation | async-start | bytes 1376256 | tf_op jit(solution)/shard_map/psum | solution.py:107
  8.0 6.5 %collective-permute-start = (bf16[1,1,8,2048]{3,2,1,0:T(8,128)(2,1)S(1)}, bf16[1,1,8,2048]{3,2,1,0:T(8,128)(2,1)S(1)}, u32[]{:S(2)}, u32[]{:S(2)}) collective-permute-start(bf16[1,1,8,2048]{3,2,1,0:T(8,128)(2,1)S(1)} %get-tuple-element.136), channel_id=1, source_target_pairs={{0,4},{4,8},{8,12},{1,5},{5,9},{9,13},{2,6},{6,10},{10,14},{3,7},{... | collective-permute-start | bytes 98312 | tf_op jit(solution)/shard_map/ppermute | solution.py:19
  12.9 5.8 %collective-permute-start.1 = (bf16[1,1,8,2048]{3,2,1,0:T(8,128)(2,1)S(1)}, bf16[1,1,8,2048]{3,2,1,0:T(8,128)(2,1)S(1)}, u32[]{:S(2)}, u32[]{:S(2)}) collective-permute-start(bf16[1,1,8,2048]{3,2,1,0:T(8,128)(2,1)S(1)} %get-tuple-element.135), channel_id=1, source_target_pairs={{4,0},{8,4},{12,8},{5,1},{9,5},{13,9},{6,2},{10,6},{14,10},{7,3},{... | collective-permute-start | bytes 98312 | tf_op jit(solution)/shard_map/ppermute | solution.py:21
  18.8 4.4 %collective-permute-start.2 = (bf16[1,4,1,2048]{3,2,1,0:T(2,128)(2,1)S(1)}, bf16[1,4,1,2048]{3,2,1,0:T(2,128)(2,1)S(1)}, u32[]{:S(2)}, u32[]{:S(2)}) collective-permute-start(bf16[1,4,1,2048]{3,2,1,0:T(2,128)(2,1)S(1)} %get-tuple-element.133), channel_id=1, source_target_pairs={{0,1},{2,3},{4,5},{6,7},{8,9},{10,11},{12,13},{14,15},{16,17},{18,... | collective-permute-start | bytes 49160 | tf_op jit(solution)/shard_map/ppermute | solution.py:19
  20.1 3.1 %collective-permute-start.3 = (bf16[1,4,1,2048]{3,2,1,0:T(2,128)(2,1)S(1)}, bf16[1,4,1,2048]{3,2,1,0:T(2,128)(2,1)S(1)}, u32[]{:S(2)}, u32[]{:S(2)}) collective-permute-start(bf16[1,4,1,2048]{3,2,1,0:T(2,128)(2,1)S(1)} %get-tuple-element.134), channel_id=1, source_target_pairs={{1,0},{3,2},{5,4},{7,6},{9,8},{11,10},{13,12},{15,14},{17,16},{19,... | collective-permute-start | bytes 49160 | tf_op jit(solution)/shard_map/ppermute | solution.py:21
  35.9 1.8 copy-start.2
  35.9 1.8 copy-start.12
  35.9 17.2 %copy-start.6 = (f32[1728,64]{0,1:T(8,128)S(1)}, f32[1728,64]{0,1:T(8,128)}, u32[]{:S(2)}) copy-start(f32[1728,64]{0,1:T(8,128)} %param.9) | copy-start | bytes 1327108
  35.9 17.9 %copy-start.10 = (bf16[1,2,8,4096]{3,2,1,0:T(8,128)(2,1)S(1)}, bf16[1,2,8,4096]{3,2,1,0:T(8,128)(2,1)}, u32[]{:S(2)}) copy-start(bf16[1,2,8,4096]{3,2,1,0:T(8,128)(2,1)} %param.11) | copy-start | bytes 393220
  39.6 5.8 %collective-permute-start.4 = (bf16[1,1,8,4096]{3,2,1,0:T(8,128)(2,1)S(1)}, bf16[1,1,8,4096]{3,2,1,0:T(8,128)(2,1)S(1)}, u32[]{:S(2)}, u32[]{:S(2)}) collective-permute-start(bf16[1,1,8,4096]{3,2,1,0:T(8,128)(2,1)S(1)} %get-tuple-element.132), channel_id=1, source_target_pairs={{0,4},{4,8},{8,12},{1,5},{5,9},{9,13},{2,6},{6,10},{10,14},{3,7},{... | collective-permute-start | bytes 196616 | tf_op jit(solution)/shard_map/ppermute | solution.py:19
  43.1 6.7 %collective-permute-start.5 = (bf16[1,1,8,4096]{3,2,1,0:T(8,128)(2,1)S(1)}, bf16[1,1,8,4096]{3,2,1,0:T(8,128)(2,1)S(1)}, u32[]{:S(2)}, u32[]{:S(2)}) collective-permute-start(bf16[1,1,8,4096]{3,2,1,0:T(8,128)(2,1)S(1)} %get-tuple-element.131), channel_id=1, source_target_pairs={{4,0},{8,4},{12,8},{5,1},{9,5},{13,9},{6,2},{10,6},{14,10},{7,3},{... | collective-permute-start | bytes 196616 | tf_op jit(solution)/shard_map/ppermute | solution.py:21
  49.9 5.0 %collective-permute-start.6 = (bf16[1,4,1,4096]{3,2,1,0:T(2,128)(2,1)S(1)}, bf16[1,4,1,4096]{3,2,1,0:T(2,128)(2,1)S(1)}, u32[]{:S(2)}, u32[]{:S(2)}) collective-permute-start(bf16[1,4,1,4096]{3,2,1,0:T(2,128)(2,1)S(1)} %get-tuple-element.125), channel_id=1, source_target_pairs={{0,1},{2,3},{4,5},{6,7},{8,9},{10,11},{12,13},{14,15},{16,17},{18,... | collective-permute-start | bytes 98312 | tf_op jit(solution)/shard_map/ppermute | solution.py:19
  51.8 3.1 %collective-permute-start.7 = (bf16[1,4,1,4096]{3,2,1,0:T(2,128)(2,1)S(1)}, bf16[1,4,1,4096]{3,2,1,0:T(2,128)(2,1)S(1)}, u32[]{:S(2)}, u32[]{:S(2)}) collective-permute-start(bf16[1,4,1,4096]{3,2,1,0:T(2,128)(2,1)S(1)} %get-tuple-element.126), channel_id=1, source_target_pairs={{1,0},{3,2},{5,4},{7,6},{9,8},{11,10},{13,12},{15,14},{17,16},{19,... | collective-permute-start | bytes 98312 | tf_op jit(solution)/shard_map/ppermute | solution.py:21
  69.7 2.5 %copy-start.1 = (bf16[1728,64]{0,1:T(8,128)(2,1)S(1)}, bf16[1728,64]{0,1:T(8,128)(2,1)}, u32[]{:S(2)}) copy-start(bf16[1728,64]{0,1:T(8,128)(2,1)} %convert_element_type.41) | copy-start | bytes 663556
  69.7 2.5 %copy-start.8 = (f32[1024,64]{0,1:T(8,128)S(1)}, f32[1024,64]{0,1:T(8,128)}, u32[]{:S(2)}) copy-start(f32[1024,64]{0,1:T(8,128)} %copy.32) | copy-start | bytes 786436
  69.7 2.5 %copy-start.13 = (f32[64]{0:T(128)S(1)}, f32[64]{0:T(128)}, u32[]{:S(2)}) copy-start(f32[64]{0:T(128)} %param.10) | copy-start | bytes 772
  72.1 2.1 copy-start
  72.2 17.5 %copy-start.3 = (bf16[864,64]{1,0:T(8,128)(2,1)S(1)}, bf16[864,64]{1,0:T(8,128)(2,1)}, u32[]{:S(2)}) copy-start(bf16[864,64]{1,0:T(8,128)(2,1)} %copy.27) | copy-start | bytes 331780
  74.2 0.7 copy-start.4
  75.4 5.8 %collective-permute-start.8 = (bf16[1,1,8,4096]{3,2,1,0:T(8,128)(2,1)S(1)}, bf16[1,1,8,4096]{3,2,1,0:T(8,128)(2,1)S(1)}, u32[]{:S(2)}, u32[]{:S(2)}) collective-permute-start(bf16[1,1,8,4096]{3,2,1,0:T(8,128)(2,1)S(1)} %get-tuple-element.130), channel_id=1, source_target_pairs={{0,4},{4,8},{8,12},{1,5},{5,9},{9,13},{2,6},{6,10},{10,14},{3,7},{... | collective-permute-start | bytes 196616 | tf_op jit(solution)/shard_map/ppermute | solution.py:19
  78.8 6.7 %collective-permute-start.9 = (bf16[1,1,8,4096]{3,2,1,0:T(8,128)(2,1)S(1)}, bf16[1,1,8,4096]{3,2,1,0:T(8,128)(2,1)S(1)}, u32[]{:S(2)}, u32[]{:S(2)}) collective-permute-start(bf16[1,1,8,4096]{3,2,1,0:T(8,128)(2,1)S(1)} %get-tuple-element.129), channel_id=1, source_target_pairs={{4,0},{8,4},{12,8},{5,1},{9,5},{13,9},{6,2},{10,6},{14,10},{7,3},{... | collective-permute-start | bytes 196616 | tf_op jit(solution)/shard_map/ppermute | solution.py:21
  86.3 8.7 %collective-permute-start.10 = (bf16[1,4,1,4096]{3,2,1,0:T(2,128)(2,1)}, bf16[1,4,1,4096]{3,2,1,0:T(2,128)(2,1)S(1)}, u32[]{:S(2)}, u32[]{:S(2)}) collective-permute-start(bf16[1,4,1,4096]{3,2,1,0:T(2,128)(2,1)} %get-tuple-element.122), channel_id=1, source_target_pairs={{0,1},{2,3},{4,5},{6,7},{8,9},{10,11},{12,13},{14,15},{16,17},{18,... | collective-permute-start | bytes 98312 | tf_op jit(solution)/shard_map/ppermute | solution.py:19
  88.2 6.8 %collective-permute-start.11 = (bf16[1,4,1,4096]{3,2,1,0:T(2,128)(2,1)S(1)}, bf16[1,4,1,4096]{3,2,1,0:T(2,128)(2,1)S(1)}, u32[]{:S(2)}, u32[]{:S(2)}) collective-permute-start(bf16[1,4,1,4096]{3,2,1,0:T(2,128)(2,1)S(1)} %get-tuple-element.123), channel_id=1, source_target_pairs={{1,0},{3,2},{5,4},{7,6},{9,8},{11,10},{13,12},{15,14},{17,16},{19,... | collective-permute-start | bytes 98312 | tf_op jit(solution)/shard_map/ppermute | solution.py:21
  109.7 2.5 %copy-start.9 = (bf16[1728,64]{0,1:T(8,128)(2,1)S(1)}, bf16[1728,64]{0,1:T(8,128)(2,1)}, u32[]{:S(2)}) copy-start(bf16[1728,64]{0,1:T(8,128)(2,1)} %reshape.78) | copy-start | bytes 663556
  109.7 2.5 %copy-start.14 = (f32[1024,64]{0,1:T(8,128)S(1)}, f32[1024,64]{0,1:T(8,128)}, u32[]{:S(2)}) copy-start(f32[1024,64]{0,1:T(8,128)} %get-tuple-element.138) | copy-start | bytes 786436
  112.1 4.2 %copy-start.5 = (bf16[1024,64]{0,1:T(8,128)(2,1)S(1)}, bf16[1024,64]{0,1:T(8,128)(2,1)}, u32[]{:S(2)}) copy-start(bf16[1024,64]{0,1:T(8,128)(2,1)} %copy-done.4) | copy-start | bytes 393220
  113.5 6.4 %copy-start.11 = (bf16[1024,64]{0,1:T(8,128)(2,1)S(1)}, bf16[1024,64]{0,1:T(8,128)(2,1)}, u32[]{:S(2)}) copy-start(bf16[1024,64]{0,1:T(8,128)(2,1)} %get-tuple-element.124) | copy-start | bytes 393220
  114.0 8.3 %collective-permute-start.12 = (bf16[1,1,8,4096]{3,2,1,0:T(8,128)(2,1)S(1)}, bf16[1,1,8,4096]{3,2,1,0:T(8,128)(2,1)S(1)}, u32[]{:S(2)}, u32[]{:S(2)}) collective-permute-start(bf16[1,1,8,4096]{3,2,1,0:T(8,128)(2,1)S(1)} %get-tuple-element.128), channel_id=1, source_target_pairs={{0,4},{4,8},{8,12},{1,5},{5,9},{9,13},{2,6},{6,10},{10,14},{3,7},{... | collective-permute-start | bytes 196616 | tf_op jit(solution)/shard_map/ppermute | solution.py:19
  121.0 6.7 %collective-permute-start.13 = (bf16[1,1,8,4096]{3,2,1,0:T(8,128)(2,1)S(1)}, bf16[1,1,8,4096]{3,2,1,0:T(8,128)(2,1)S(1)}, u32[]{:S(2)}, u32[]{:S(2)}) collective-permute-start(bf16[1,1,8,4096]{3,2,1,0:T(8,128)(2,1)S(1)} %get-tuple-element.127), channel_id=1, source_target_pairs={{4,0},{8,4},{12,8},{5,1},{9,5},{13,9},{6,2},{10,6},{14,10},{7,3},{... | collective-permute-start | bytes 196616 | tf_op jit(solution)/shard_map/ppermute | solution.py:21
  127.8 35.6 %collective-permute-start.14 = (bf16[1,4,1,4096]{3,2,1,0:T(2,128)(2,1)S(1)}, bf16[1,4,1,4096]{3,2,1,0:T(2,128)(2,1)S(1)}, u32[]{:S(2)}, u32[]{:S(2)}) collective-permute-start(bf16[1,4,1,4096]{3,2,1,0:T(2,128)(2,1)S(1)} %get-tuple-element.120), channel_id=1, source_target_pairs={{0,1},{2,3},{4,5},{6,7},{8,9},{10,11},{12,13},{14,15},{16,17},{18,... | collective-permute-start | bytes 98312 | tf_op jit(solution)/shard_map/ppermute | solution.py:19
  129.7 33.7 %collective-permute-start.15 = (bf16[1,4,1,4096]{3,2,1,0:T(2,128)(2,1)S(1)}, bf16[1,4,1,4096]{3,2,1,0:T(2,128)(2,1)S(1)}, u32[]{:S(2)}, u32[]{:S(2)}) collective-permute-start(bf16[1,4,1,4096]{3,2,1,0:T(2,128)(2,1)S(1)} %get-tuple-element.121), channel_id=1, source_target_pairs={{1,0},{3,2},{5,4},{7,6},{9,8},{11,10},{13,12},{15,14},{17,16},{19,... | collective-permute-start | bytes 98312 | tf_op jit(solution)/shard_map/ppermute | solution.py:21
  177.2 2.4 %copy-start.7 = (bf16[1728,32]{0,1:T(8,128)(2,1)S(1)}, bf16[1728,32]{0,1:T(8,128)(2,1)}, u32[]{:S(2)}) copy-start(bf16[1728,32]{0,1:T(8,128)(2,1)} %reshape.83) | copy-start | bytes 331780
Sparse Core Ops, SparseCore 0:
  132.2 91.0 all-reduce.7
where the time goes:
time: 237 us; the launch traced here: 234 us
  local copies, waits for them, and re-layouts  82.5 us (35%)
  waiting for transfers between devices  61.4 us (26%)
  starting transfers between devices  31.7 us (13%)
  blocking collectives  31.3 us (13%)
  between operations  14.7 us (6%)
  matrix products  10.6 us (4%)
    concatenate x8, local copies, waits for them, and re-layouts, columns(): return jnp.concatenate(pieces, axis=-1).reshape(-1, 27 * chans)  44 us
    psum x1, waiting for transfers between devices, on_device(): lax.psum((grad_w1, grad_b1, grad_w2, grad_b2), ('space', 'dp', 'ysp'))  41.4 us
    psum x1, blocking collectives, on_device(): lax.psum((grad_w1, grad_b1, grad_w2, grad_b2), ('space', 'dp', 'ysp'))  31.3 us
    ppermute x8, starting transfers between devices, padded_2(): lax.ppermute(tail, axis, [(i, (i + 1) % count) for i in range(ends)])  21.1 us
    ppermute x8, waiting for transfers between devices, padded_2(): lax.ppermute(head, axis, [((i + 1) % count, i) for i in range(ends)])  17.6 us
    slice x12, local copies, waits for them, and re-layouts, columns(): cells[:, first:first + wide_x, second:second + wide_y, third:third + DEPT...  17.1 us
    ppermute x8, starting transfers between devices, padded_2(): lax.ppermute(head, axis, [((i + 1) % count, i) for i in range(ends)])  10.5 us
    unnamed x41, local copies, waits for them, and re-layouts  6.87 us
  transfers between devices with their start and end apart: 17, of which 8 were waited for; matrix products, arithmetic and copies ran while one was open for 15% of the time, Pallas kernels for 0%

commit v1 on v0

--- a/solution.py
+++ b/solution.py
@@ -105,7 +105,7 @@
     )
     input_grad = d_input.astype(jnp.bfloat16).reshape(batch, cells_x, cells_y, DEPTH * C_IN)
     grad_w1, grad_b1, grad_w2, grad_b2 = lax.psum(
-        (grad_w1, grad_b1, grad_w2, grad_b2), ("space", "dp", "ysp")
+        lax.psum((grad_w1, grad_b1, grad_w2, grad_b2), axis_name=("dp", "ysp")), axis_name="space"
     )
     return (output, input_grad, grad_w1, grad_b1, grad_w2, grad_b2)
 

time: 237 us -> 224 us (0.945)
  blocking collectives: 31.3 us -> 17.1 us
    psum x1 -> x2, blocking collectives: 31.3 us -> 17.1 us  [the longest x1 8.86 us: on_device(): lax.psum(lax.psum((grad_w1, grad_b1, grad_w2, grad_b2), axis_name=('dp',...]
    psum x1 -> x2, waiting for transfers between devices: 41.4 us -> 41.8 us  [the longest x1 27.6 us: on_device(): lax.psum(lax.psum((grad_w1, grad_b1, grad_w2, grad_b2), axis_name=('dp',...]
  transfers between devices with their start and end apart: 17 -> 18, of which waited for: 8 -> 9; matrix products, arithmetic and copies ran while one was open for 15% -> 16% of each run, Pallas kernels for 0% -> 0%
where the time goes in v1:
time: 224 us; the launch traced here: 220 us
  local copies, waits for them, and re-layouts  82.6 us (37%)
  waiting for transfers between devices  61.7 us (28%)
  starting transfers between devices  31.7 us (14%)
  blocking collectives  17.1 us (8%)
  between operations  14.7 us (7%)
  matrix products  10.6 us (5%)
    concatenate x8, local copies, waits for them, and re-layouts, columns(): return jnp.concatenate(pieces, axis=-1).reshape(-1, 27 * chans)  44.2 us
    psum x1, waiting for transfers between devices, on_device(): lax.psum(lax.psum((grad_w1, grad_b1, grad_w2, grad_b2), axis_name=('dp',...  27.6 us
    ppermute x8, starting transfers between devices, padded_2(): lax.ppermute(tail, axis, [(i, (i + 1) % count) for i in range(ends)])  21.1 us
    ppermute x8, waiting for transfers between devices, padded_2(): lax.ppermute(head, axis, [((i + 1) % count, i) for i in range(ends)])  17.6 us
    slice x12, local copies, waits for them, and re-layouts, columns(): cells[:, first:first + wide_x, second:second + wide_y, third:third + DEPT...  17 us
    psum x1, waiting for transfers between devices, on_device(): lax.psum((grad_w1, grad_b1, grad_w2, grad_b2), axis_name=('dp', 'ysp'))  14.2 us
    ppermute x8, starting transfers between devices, padded_2(): lax.ppermute(head, axis, [((i + 1) % count, i) for i in range(ends)])  10.5 us
    psum x1, blocking collectives, on_device(): lax.psum(lax.psum((grad_w1, grad_b1, grad_w2, grad_b2), axis_name=('dp',...  8.86 us
  transfers between devices with their start and end apart: 18, of which 9 were waited for; matrix products, arithmetic and copies ran while one was open for 16% of the time, Pallas kernels for 0%

profile of v1, /device:TPU:0, one launch (start us, length us, event | category | flops | bytes accessed | tf_op | source)
XLA Modules:
  0.0 220.0 jit_solution(1219700791891693101)
XLA Ops:
  8.0 4.9 %collective-permute-start = (bf16[1,1,8,2048]{3,2,1,0:T(8,128)(2,1)S(1)}, bf16[1,1,8,2048]{3,2,1,0:T(8,128)(2,1)S(1)}, u32[]{:S(2)}, u32[]{:S(2)}) collective-permute-start(bf16[1,1,8,2048]{3,2,1,0:T(8,128)(2,1)S(1)} %get-tuple-element.140), channel_id=1, source_target_pairs={{0,4},{4,8},{8,12},{1,5},{5,9},{9,13},{2,6},{6,10},{10,14},{3,7},{... | collective-permute-start | bytes 98312 | tf_op jit(solution)/shard_map/ppermute | solution.py:19
  12.9 1.3 collective-permute-start.1
  15.3 3.4 %collective-permute-done.1 = bf16[1,1,8,2048]{3,2,1,0:T(8,128)(2,1)S(1)} collective-permute-done((bf16[1,1,8,2048]{3,2,1,0:T(8,128)(2,1)S(1)}, bf16[1,1,8,2048]{3,2,1,0:T(8,128)(2,1)S(1)}, u32[]{:S(2)}, u32[]{:S(2)}) %collective-permute-start.1) | collective-permute-done | bytes 32800 | tf_op jit(solution)/shard_map/ppermute | solution.py:21
  18.8 1.3 collective-permute-start.2
  20.1 1.3 collective-permute-start.3
  21.4 1.8 copy.27
  24.2 1.6 pad_slice_fusion.54
  25.8 1.8 pad_slice_fusion.55
  27.5 8.3 %concatenate.38 = bf16[1,2,8,64,864]{4,3,1,2,0:T(8,128)(2,1)} concatenate(bf16[1,2,8,64,32]{4,3,1,2,0:T(8,128)(2,1)S(1)} %get-tuple-element.123, bf16[1,2,8,64,32]{4,3,1,2,0:T(8,128)(2,1)S(1)} %get-tuple-element.122, bf16[1,2,8,64,32]{4,3,1,2,0:T(8,128)(2,1)S(1)} %get-tuple-element.98, bf16[1,2,8,64,32]{4,3,1,2,0:T(8,128)(2,1)S(1)} %get-tuple-element.99, ...), dimensions={4} | concatenate | bytes 3538944 | tf_op jit(solution)/shard_map/concatenate | solution.py:47
  35.9 1.7 copy.26
  37.7 1.4 multiply_convert_fusion.2
  39.6 3.5 %collective-permute-start.4 = (bf16[1,1,8,4096]{3,2,1,0:T(8,128)(2,1)S(1)}, bf16[1,1,8,4096]{3,2,1,0:T(8,128)(2,1)S(1)}, u32[]{:S(2)}, u32[]{:S(2)}) collective-permute-start(bf16[1,1,8,4096]{3,2,1,0:T(8,128)(2,1)S(1)} %get-tuple-element.136), channel_id=1, source_target_pairs={{0,4},{4,8},{8,12},{1,5},{5,9},{9,13},{2,6},{6,10},{10,14},{3,7},{... | collective-permute-start | bytes 196616 | tf_op jit(solution)/shard_map/ppermute | solution.py:19
  43.1 1.3 collective-permute-start.5
  45.4 4.4 %collective-permute-done.5 = bf16[1,1,8,4096]{3,2,1,0:T(8,128)(2,1)S(1)} collective-permute-done((bf16[1,1,8,4096]{3,2,1,0:T(8,128)(2,1)S(1)}, bf16[1,1,8,4096]{3,2,1,0:T(8,128)(2,1)S(1)}, u32[]{:S(2)}, u32[]{:S(2)}) %collective-permute-start.5) | collective-permute-done | bytes 65568 | tf_op jit(solution)/shard_map/ppermute | solution.py:21
  49.9 1.9 collective-permute-start.6
  51.8 1.3 collective-permute-start.7
  57.2 1.9 pad_slice_fusion.36
  59.0 1.8 pad_slice_fusion.37
  60.8 8.8 %concatenate.41 = bf16[1,2,8,64,1728]{4,3,1,2,0:T(8,128)(2,1)} concatenate(bf16[1,2,8,64,64]{4,3,1,2,0:T(8,128)(2,1)} %get-tuple-element.96, bf16[1,2,8,64,64]{4,3,1,2,0:T(8,128)(2,1)} %get-tuple-element.95, bf16[1,2,8,64,64]{4,3,1,2,0:T(8,128)(2,1)} %get-tuple-element.71, bf16[1,2,8,64,64]{4,3,1,2,0:T(8,128)(2,1)} %get-tuple-element.72, ...), dimensions={4} | concatenate | bytes 7077888 | tf_op jit(solution)/shard_map/concatenate | solution.py:47
  69.7 2.4 %copy.30 = bf16[1,2,8,64,1728]{4,3,2,1,0:T(8,128)(2,1)S(1)} copy(bf16[1,2,8,64,1728]{4,3,1,2,0:T(8,128)(2,1)} %concatenate.41) | data formatting | bytes 7077888 | tf_op jit(solution)/shard_map/concatenate | solution.py:47
  72.2 2.0 convert_reduce_fusion
  75.4 3.5 %collective-permute-start.8 = (bf16[1,1,8,4096]{3,2,1,0:T(8,128)(2,1)S(1)}, bf16[1,1,8,4096]{3,2,1,0:T(8,128)(2,1)S(1)}, u32[]{:S(2)}, u32[]{:S(2)}) collective-permute-start(bf16[1,1,8,4096]{3,2,1,0:T(8,128)(2,1)S(1)} %get-tuple-element.134), channel_id=1, source_target_pairs={{0,4},{4,8},{8,12},{1,5},{5,9},{9,13},{2,6},{6,10},{10,14},{3,7},{... | collective-permute-start | bytes 196616 | tf_op jit(solution)/shard_map/ppermute | solution.py:19
  78.8 1.3 collective-permute-start.9
  81.2 4.4 %collective-permute-done.9 = bf16[1,1,8,4096]{3,2,1,0:T(8,128)(2,1)S(1)} collective-permute-done((bf16[1,1,8,4096]{3,2,1,0:T(8,128)(2,1)S(1)}, bf16[1,1,8,4096]{3,2,1,0:T(8,128)(2,1)S(1)}, u32[]{:S(2)}, u32[]{:S(2)}) %collective-permute-start.9) | collective-permute-done | bytes 65568 | tf_op jit(solution)/shard_map/ppermute | solution.py:21
  86.3 1.9 collective-permute-start.10
  88.2 1.5 collective-permute-start.11
  91.1 1.7 rev.6
  97.2 1.8 pad_slice_fusion.18
  99.1 1.8 pad_slice_fusion.19
  100.8 8.8 %concatenate.44 = bf16[1,2,8,64,1728]{4,3,1,2,0:T(8,128)(2,1)} concatenate(bf16[1,2,8,64,64]{4,3,1,2,0:T(8,128)(2,1)} %get-tuple-element.69, bf16[1,2,8,64,64]{4,3,1,2,0:T(8,128)(2,1)} %get-tuple-element.68, bf16[1,2,8,64,64]{4,3,1,2,0:T(8,128)(2,1)} %get-tuple-element.44, bf16[1,2,8,64,64]{4,3,1,2,0:T(8,128)(2,1)} %get-tuple-element.45, ...), dimensions={4} | concatenate | bytes 7077888 | tf_op jit(solution)/shard_map/concatenate | solution.py:47
  109.7 2.4 %copy.35 = bf16[1,2,8,64,1728]{4,3,2,1,0:T(8,128)(2,1)S(1)} copy(bf16[1,2,8,64,1728]{4,3,1,2,0:T(8,128)(2,1)} %concatenate.44) | data formatting | bytes 7077888 | tf_op jit(solution)/shard_map/concatenate | solution.py:47
  112.2 1.3 convert_reduce_fusion.1
  114.0 2.3 %collective-permute-start.12 = (bf16[1,1,8,4096]{3,2,1,0:T(8,128)(2,1)S(1)}, bf16[1,1,8,4096]{3,2,1,0:T(8,128)(2,1)S(1)}, u32[]{:S(2)}, u32[]{:S(2)}) collective-permute-start(bf16[1,1,8,4096]{3,2,1,0:T(8,128)(2,1)S(1)} %get-tuple-element.132), channel_id=1, source_target_pairs={{0,4},{4,8},{8,12},{1,5},{5,9},{9,13},{2,6},{6,10},{10,14},{3,7},{... | collective-permute-start | bytes 196616 | tf_op jit(solution)/shard_map/ppermute | solution.py:19
  116.3 3.6 %fusion.14 = f32[1728,64]{0,1:T(8,128)} fusion(bf16[1024,64]{0,1:T(8,128)(2,1)S(1)} %copy-done.5, bf16[1024,1728]{1,0:T(8,128)(2,1)} %bitcast.38), kind=kOutput, calls=%fused_computation.114 | convolution fusion | flops 226492416 | bytes 4112384 | tf_op jit(solution)/shard_map/dot_general | solution.py:61
  121.0 1.3 collective-permute-start.13
  122.3 5.4 %collective-permute-done.13 = bf16[1,1,8,4096]{3,2,1,0:T(8,128)(2,1)S(1)} collective-permute-done((bf16[1,1,8,4096]{3,2,1,0:T(8,128)(2,1)S(1)}, bf16[1,1,8,4096]{3,2,1,0:T(8,128)(2,1)S(1)}, u32[]{:S(2)}, u32[]{:S(2)}) %collective-permute-start.13) | collective-permute-done | bytes 65568 | tf_op jit(solution)/shard_map/ppermute | solution.py:21
  127.8 1.9 collective-permute-start.14
  129.7 1.3 collective-permute-start.15
  132.2 8.2 %all-reduce.4 = (f32[64]{0:T(128)S(1)}, f32[64]{0:T(128)S(1)}) all-reduce(f32[64]{0:T(128)S(1)} %get-tuple-element.143, f32[64]{0:T(128)S(1)} %get-tuple-element.14), channel_id=1, replica_groups=mesh['groups'=2,'space'=4,'dp'=2,'ysp'=2] {'dp','ysp'}, use_global_device_ids=true, to_apply=%region_3.4 | all-reduce | flops 128 | bytes 1024 | tf_op jit(solution)/shard_map/psum | solution.py:108
  140.4 8.9 %all-reduce.6 = (f32[64]{0:T(128)}, f32[64]{0:T(128)}) all-reduce(f32[64]{0:T(128)S(1)} %get-tuple-element.6, f32[64]{0:T(128)S(1)} %get-tuple-element.7), channel_id=1, replica_groups=mesh['groups'=2,'space'=4,'dp'=2,'ysp'=2] {'space'}, use_global_device_ids=true, to_apply=%region_4.5 | all-reduce | flops 128 | bytes 1024 | tf_op jit(solution)/shard_map/psum | solution.py:107
  151.1 14.2 %all-reduce.11.cloned.1.call-done = (f32[864,64]{0,1:T(8,128)}, f32[1728,64]{0,1:T(8,128)}) async-done(((f32[864,64]{0,1:T(8,128)}, f32[1728,64]{0,1:T(8,128)}), (f32[864,64]{0,1:T(8,128)}, f32[1728,64]{0,1:T(8,128)})) %all-reduce.11.cloned.1.call-update) | async-done | bytes 663568 | tf_op jit(solution)/shard_map/psum | solution.py:108
  165.3 1.2 fusion.1
  166.5 1.7 pad_slice_fusion.1
  168.2 9.2 %concatenate.47 = bf16[1,2,8,64,1728]{4,3,1,2,0:T(8,128)(2,1)} concatenate(bf16[1,2,8,64,64]{4,3,1,2,0:T(8,128)(2,1)} %get-tuple-element.42, bf16[1,2,8,64,64]{4,3,1,2,0:T(8,128)(2,1)} %get-tuple-element.41, bf16[1,2,8,64,64]{4,3,1,2,0:T(8,128)(2,1)S(1)} %get-tuple-element.17, bf16[1,2,8,64,64]{4,3,1,2,0:T(8,128)(2,1)S(1)} %get-tuple-element.18, ...), dimensions={4} | concatenate | bytes 7077888 | tf_op jit(solution)/shard_map/concatenate | solution.py:47
  177.4 2.4 %copy.39 = bf16[1,2,8,64,1728]{4,3,2,1,0:T(8,128)(2,1)S(1)} copy(bf16[1,2,8,64,1728]{4,3,1,2,0:T(8,128)(2,1)} %concatenate.47) | data formatting | bytes 7077888 | tf_op jit(solution)/shard_map/concatenate | solution.py:47
  182.1 27.6 %all-reduce.13.cloned.1.call-done = (f32[864,64]{0,1:T(8,128)}, f32[1728,64]{0,1:T(8,128)}) async-done(((f32[864,64]{0,1:T(8,128)}, f32[1728,64]{0,1:T(8,128)}), (f32[864,64]{0,1:T(8,128)}, f32[1728,64]{0,1:T(8,128)})) %all-reduce.13.cloned.1.call-update) | async-done | bytes 663568 | tf_op jit(solution)/shard_map/psum | solution.py:107
  209.7 1.6 copy.54
  211.4 1.8 copy.55
  (103 shorter events, 24.2 us)
Async XLA Ops:
  7.2 158.1 %all-reduce.11.cloned.1.call-start = ((), (), s32[]{:S(2)}) async-start(), calls=%async_computation | async-start | bytes 1376256 | tf_op jit(solution)/shard_map/psum | solution.py:108
  8.0 6.5 %collective-permute-start = (bf16[1,1,8,2048]{3,2,1,0:T(8,128)(2,1)S(1)}, bf16[1,1,8,2048]{3,2,1,0:T(8,128)(2,1)S(1)}, u32[]{:S(2)}, u32[]{:S(2)}) collective-permute-start(bf16[1,1,8,2048]{3,2,1,0:T(8,128)(2,1)S(1)} %get-tuple-element.140), channel_id=1, source_target_pairs={{0,4},{4,8},{8,12},{1,5},{5,9},{9,13},{2,6},{6,10},{10,14},{3,7},{... | collective-permute-start | bytes 98312 | tf_op jit(solution)/shard_map/ppermute | solution.py:19
  12.9 5.8 %collective-permute-start.1 = (bf16[1,1,8,2048]{3,2,1,0:T(8,128)(2,1)S(1)}, bf16[1,1,8,2048]{3,2,1,0:T(8,128)(2,1)S(1)}, u32[]{:S(2)}, u32[]{:S(2)}) collective-permute-start(bf16[1,1,8,2048]{3,2,1,0:T(8,128)(2,1)S(1)} %get-tuple-element.139), channel_id=1, source_target_pairs={{4,0},{8,4},{12,8},{5,1},{9,5},{13,9},{6,2},{10,6},{14,10},{7,3},{... | collective-permute-start | bytes 98312 | tf_op jit(solution)/shard_map/ppermute | solution.py:21
  18.8 4.4 %collective-permute-start.2 = (bf16[1,4,1,2048]{3,2,1,0:T(2,128)(2,1)S(1)}, bf16[1,4,1,2048]{3,2,1,0:T(2,128)(2,1)S(1)}, u32[]{:S(2)}, u32[]{:S(2)}) collective-permute-start(bf16[1,4,1,2048]{3,2,1,0:T(2,128)(2,1)S(1)} %get-tuple-element.137), channel_id=1, source_target_pairs={{0,1},{2,3},{4,5},{6,7},{8,9},{10,11},{12,13},{14,15},{16,17},{18,... | collective-permute-start | bytes 49160 | tf_op jit(solution)/shard_map/ppermute | solution.py:19
  20.1 3.1 %collective-permute-start.3 = (bf16[1,4,1,2048]{3,2,1,0:T(2,128)(2,1)S(1)}, bf16[1,4,1,2048]{3,2,1,0:T(2,128)(2,1)S(1)}, u32[]{:S(2)}, u32[]{:S(2)}) collective-permute-start(bf16[1,4,1,2048]{3,2,1,0:T(2,128)(2,1)S(1)} %get-tuple-element.138), channel_id=1, source_target_pairs={{1,0},{3,2},{5,4},{7,6},{9,8},{11,10},{13,12},{15,14},{17,16},{19,... | collective-permute-start | bytes 49160 | tf_op jit(solution)/shard_map/ppermute | solution.py:21
  35.9 1.8 copy-start.2
  35.9 1.8 copy-start.12
  35.9 17.2 %copy-start.6 = (f32[1728,64]{0,1:T(8,128)S(1)}, f32[1728,64]{0,1:T(8,128)}, u32[]{:S(2)}) copy-start(f32[1728,64]{0,1:T(8,128)} %param.9) | copy-start | bytes 1327108
  35.9 17.9 %copy-start.10 = (bf16[1,2,8,4096]{3,2,1,0:T(8,128)(2,1)S(1)}, bf16[1,2,8,4096]{3,2,1,0:T(8,128)(2,1)}, u32[]{:S(2)}) copy-start(bf16[1,2,8,4096]{3,2,1,0:T(8,128)(2,1)} %param.11) | copy-start | bytes 393220
  39.6 5.8 %collective-permute-start.4 = (bf16[1,1,8,4096]{3,2,1,0:T(8,128)(2,1)S(1)}, bf16[1,1,8,4096]{3,2,1,0:T(8,128)(2,1)S(1)}, u32[]{:S(2)}, u32[]{:S(2)}) collective-permute-start(bf16[1,1,8,4096]{3,2,1,0:T(8,128)(2,1)S(1)} %get-tuple-element.136), channel_id=1, source_target_pairs={{0,4},{4,8},{8,12},{1,5},{5,9},{9,13},{2,6},{6,10},{10,14},{3,7},{... | collective-permute-start | bytes 196616 | tf_op jit(solution)/shard_map/ppermute | solution.py:19
  43.1 6.7 %collective-permute-start.5 = (bf16[1,1,8,4096]{3,2,1,0:T(8,128)(2,1)S(1)}, bf16[1,1,8,4096]{3,2,1,0:T(8,128)(2,1)S(1)}, u32[]{:S(2)}, u32[]{:S(2)}) collective-permute-start(bf16[1,1,8,4096]{3,2,1,0:T(8,128)(2,1)S(1)} %get-tuple-element.135), channel_id=1, source_target_pairs={{4,0},{8,4},{12,8},{5,1},{9,5},{13,9},{6,2},{10,6},{14,10},{7,3},{... | collective-permute-start | bytes 196616 | tf_op jit(solution)/shard_map/ppermute | solution.py:21
  49.9 5.0 %collective-permute-start.6 = (bf16[1,4,1,4096]{3,2,1,0:T(2,128)(2,1)S(1)}, bf16[1,4,1,4096]{3,2,1,0:T(2,128)(2,1)S(1)}, u32[]{:S(2)}, u32[]{:S(2)}) collective-permute-start(bf16[1,4,1,4096]{3,2,1,0:T(2,128)(2,1)S(1)} %get-tuple-element.129), channel_id=1, source_target_pairs={{0,1},{2,3},{4,5},{6,7},{8,9},{10,11},{12,13},{14,15},{16,17},{18,... | collective-permute-start | bytes 98312 | tf_op jit(solution)/shard_map/ppermute | solution.py:19
  51.8 3.1 %collective-permute-start.7 = (bf16[1,4,1,4096]{3,2,1,0:T(2,128)(2,1)S(1)}, bf16[1,4,1,4096]{3,2,1,0:T(2,128)(2,1)S(1)}, u32[]{:S(2)}, u32[]{:S(2)}) collective-permute-start(bf16[1,4,1,4096]{3,2,1,0:T(2,128)(2,1)S(1)} %get-tuple-element.130), channel_id=1, source_target_pairs={{1,0},{3,2},{5,4},{7,6},{9,8},{11,10},{13,12},{15,14},{17,16},{19,... | collective-permute-start | bytes 98312 | tf_op jit(solution)/shard_map/ppermute | solution.py:21
  69.7 2.5 %copy-start.1 = (bf16[1728,64]{0,1:T(8,128)(2,1)S(1)}, bf16[1728,64]{0,1:T(8,128)(2,1)}, u32[]{:S(2)}) copy-start(bf16[1728,64]{0,1:T(8,128)(2,1)} %convert_element_type.41) | copy-start | bytes 663556
  69.7 2.5 %copy-start.8 = (f32[1024,64]{0,1:T(8,128)S(1)}, f32[1024,64]{0,1:T(8,128)}, u32[]{:S(2)}) copy-start(f32[1024,64]{0,1:T(8,128)} %copy.32) | copy-start | bytes 786436
  69.7 2.5 %copy-start.13 = (f32[64]{0:T(128)S(1)}, f32[64]{0:T(128)}, u32[]{:S(2)}) copy-start(f32[64]{0:T(128)} %param.10) | copy-start | bytes 772
  72.1 2.1 copy-start
  72.2 17.5 %copy-start.3 = (bf16[864,64]{1,0:T(8,128)(2,1)S(1)}, bf16[864,64]{1,0:T(8,128)(2,1)}, u32[]{:S(2)}) copy-start(bf16[864,64]{1,0:T(8,128)(2,1)} %copy.27) | copy-start | bytes 331780
  74.2 0.7 copy-start.4
  75.4 5.8 %collective-permute-start.8 = (bf16[1,1,8,4096]{3,2,1,0:T(8,128)(2,1)S(1)}, bf16[1,1,8,4096]{3,2,1,0:T(8,128)(2,1)S(1)}, u32[]{:S(2)}, u32[]{:S(2)}) collective-permute-start(bf16[1,1,8,4096]{3,2,1,0:T(8,128)(2,1)S(1)} %get-tuple-element.134), channel_id=1, source_target_pairs={{0,4},{4,8},{8,12},{1,5},{5,9},{9,13},{2,6},{6,10},{10,14},{3,7},{... | collective-permute-start | bytes 196616 | tf_op jit(solution)/shard_map/ppermute | solution.py:19
  78.8 6.7 %collective-permute-start.9 = (bf16[1,1,8,4096]{3,2,1,0:T(8,128)(2,1)S(1)}, bf16[1,1,8,4096]{3,2,1,0:T(8,128)(2,1)S(1)}, u32[]{:S(2)}, u32[]{:S(2)}) collective-permute-start(bf16[1,1,8,4096]{3,2,1,0:T(8,128)(2,1)S(1)} %get-tuple-element.133), channel_id=1, source_target_pairs={{4,0},{8,4},{12,8},{5,1},{9,5},{13,9},{6,2},{10,6},{14,10},{7,3},{... | collective-permute-start | bytes 196616 | tf_op jit(solution)/shard_map/ppermute | solution.py:21
  86.3 8.7 %collective-permute-start.10 = (bf16[1,4,1,4096]{3,2,1,0:T(2,128)(2,1)}, bf16[1,4,1,4096]{3,2,1,0:T(2,128)(2,1)S(1)}, u32[]{:S(2)}, u32[]{:S(2)}) collective-permute-start(bf16[1,4,1,4096]{3,2,1,0:T(2,128)(2,1)} %get-tuple-element.126), channel_id=1, source_target_pairs={{0,1},{2,3},{4,5},{6,7},{8,9},{10,11},{12,13},{14,15},{16,17},{18,... | collective-permute-start | bytes 98312 | tf_op jit(solution)/shard_map/ppermute | solution.py:19
  88.2 6.8 %collective-permute-start.11 = (bf16[1,4,1,4096]{3,2,1,0:T(2,128)(2,1)S(1)}, bf16[1,4,1,4096]{3,2,1,0:T(2,128)(2,1)S(1)}, u32[]{:S(2)}, u32[]{:S(2)}) collective-permute-start(bf16[1,4,1,4096]{3,2,1,0:T(2,128)(2,1)S(1)} %get-tuple-element.127), channel_id=1, source_target_pairs={{1,0},{3,2},{5,4},{7,6},{9,8},{11,10},{13,12},{15,14},{17,16},{19,... | collective-permute-start | bytes 98312 | tf_op jit(solution)/shard_map/ppermute | solution.py:21
  109.7 2.5 %copy-start.9 = (bf16[1728,64]{0,1:T(8,128)(2,1)S(1)}, bf16[1728,64]{0,1:T(8,128)(2,1)}, u32[]{:S(2)}) copy-start(bf16[1728,64]{0,1:T(8,128)(2,1)} %reshape.78) | copy-start | bytes 663556
  109.7 2.5 %copy-start.14 = (f32[1024,64]{0,1:T(8,128)S(1)}, f32[1024,64]{0,1:T(8,128)}, u32[]{:S(2)}) copy-start(f32[1024,64]{0,1:T(8,128)} %get-tuple-element.142) | copy-start | bytes 786436
  112.1 4.2 %copy-start.5 = (bf16[1024,64]{0,1:T(8,128)(2,1)S(1)}, bf16[1024,64]{0,1:T(8,128)(2,1)}, u32[]{:S(2)}) copy-start(bf16[1024,64]{0,1:T(8,128)(2,1)} %copy-done.4) | copy-start | bytes 393220
  113.5 6.4 %copy-start.11 = (bf16[1024,64]{0,1:T(8,128)(2,1)S(1)}, bf16[1024,64]{0,1:T(8,128)(2,1)}, u32[]{:S(2)}) copy-start(bf16[1024,64]{0,1:T(8,128)(2,1)} %get-tuple-element.128) | copy-start | bytes 393220
  114.0 8.3 %collective-permute-start.12 = (bf16[1,1,8,4096]{3,2,1,0:T(8,128)(2,1)S(1)}, bf16[1,1,8,4096]{3,2,1,0:T(8,128)(2,1)S(1)}, u32[]{:S(2)}, u32[]{:S(2)}) collective-permute-start(bf16[1,1,8,4096]{3,2,1,0:T(8,128)(2,1)S(1)} %get-tuple-element.132), channel_id=1, source_target_pairs={{0,4},{4,8},{8,12},{1,5},{5,9},{9,13},{2,6},{6,10},{10,14},{3,7},{... | collective-permute-start | bytes 196616 | tf_op jit(solution)/shard_map/ppermute | solution.py:19
  121.0 6.7 %collective-permute-start.13 = (bf16[1,1,8,4096]{3,2,1,0:T(8,128)(2,1)S(1)}, bf16[1,1,8,4096]{3,2,1,0:T(8,128)(2,1)S(1)}, u32[]{:S(2)}, u32[]{:S(2)}) collective-permute-start(bf16[1,1,8,4096]{3,2,1,0:T(8,128)(2,1)S(1)} %get-tuple-element.131), channel_id=1, source_target_pairs={{4,0},{8,4},{12,8},{5,1},{9,5},{13,9},{6,2},{10,6},{14,10},{7,3},{... | collective-permute-start | bytes 196616 | tf_op jit(solution)/shard_map/ppermute | solution.py:21
  127.8 21.5 %collective-permute-start.14 = (bf16[1,4,1,4096]{3,2,1,0:T(2,128)(2,1)S(1)}, bf16[1,4,1,4096]{3,2,1,0:T(2,128)(2,1)S(1)}, u32[]{:S(2)}, u32[]{:S(2)}) collective-permute-start(bf16[1,4,1,4096]{3,2,1,0:T(2,128)(2,1)S(1)} %get-tuple-element.124), channel_id=1, source_target_pairs={{0,1},{2,3},{4,5},{6,7},{8,9},{10,11},{12,13},{14,15},{16,17},{18,... | collective-permute-start | bytes 98312 | tf_op jit(solution)/shard_map/ppermute | solution.py:19
  129.7 19.6 %collective-permute-start.15 = (bf16[1,4,1,4096]{3,2,1,0:T(2,128)(2,1)S(1)}, bf16[1,4,1,4096]{3,2,1,0:T(2,128)(2,1)S(1)}, u32[]{:S(2)}, u32[]{:S(2)}) collective-permute-start(bf16[1,4,1,4096]{3,2,1,0:T(2,128)(2,1)S(1)} %get-tuple-element.125), channel_id=1, source_target_pairs={{1,0},{3,2},{5,4},{7,6},{9,8},{11,10},{13,12},{15,14},{17,16},{19,... | collective-permute-start | bytes 98312 | tf_op jit(solution)/shard_map/ppermute | solution.py:21
  132.1 77.6 %all-reduce.13.cloned.1.call-start = ((), (), s32[]{:S(2)}) async-start(), calls=%async_computation.1 | async-start | bytes 1376256 | tf_op jit(solution)/shard_map/psum | solution.py:107
  177.4 2.5 %copy-start.7 = (bf16[1728,32]{0,1:T(8,128)(2,1)S(1)}, bf16[1728,32]{0,1:T(8,128)(2,1)}, u32[]{:S(2)}) copy-start(bf16[1728,32]{0,1:T(8,128)(2,1)} %reshape.83) | copy-start | bytes 331780
Sparse Core Ops, SparseCore 0:
  132.2 32.9 all-reduce.10
  167.8 41.8 all-reduce.12
